TPU v7x, 256 devices: a whole 4x4x8 slice. The times are simulated.
256 devices in a mesh: seq: 32 (over y_hi, z, core), head: 8 (over y_lo, x).
Axes of the slice: x: 4, y: 4 (y_hi: 2, y_lo: 2; y = y_hi * 2 + y_lo), z: 8, core: 2. Of those that a mesh axis runs over, the one named last changes fastest.
Arguments:
- q_cells: bfloat16 [8192, 8192], P('seq', 'head'), may hold values from -60 to 60
- k_cells: bfloat16 [8192, 1024], P('seq', 'head'), may hold values from -11 to 11
- v_cells: bfloat16 [8192, 1024], P('seq', 'head'), may hold values from -6 to 6
- do_cells: bfloat16 [8192, 8192], P('seq', 'head'), may hold values from -6 to 6
- q_head: bfloat16 [1024, 8192], P('seq', 'head'), may hold values from -60 to 60
- k_head: bfloat16 [1024, 1024], P('seq', 'head'), may hold values from -6 to 6
- v_head: bfloat16 [1024, 1024], P('seq', 'head'), may hold values from -6 to 6
- do_head: bfloat16 [1024, 8192], P('seq', 'head'), may hold values from -6 to 6
- vis_mask: int32 [64, 8], P('seq'), may hold values from 0 to 1, as said below
Outputs:
- dq_cells: bfloat16 [8192, 8192], P('seq', 'head')
- dk_cells: bfloat16 [8192, 1024], P('seq', 'head')
- dv_cells: bfloat16 [8192, 1024], P('seq', 'head')
- dq_head: bfloat16 [1024, 8192], P('seq', 'head')
- dk_head: bfloat16 [1024, 1024], P('seq', 'head')
- dv_head: bfloat16 [1024, 1024], P('seq', 'head')
Inputs may be any that keep to these rules, and one draw needn't show every extreme that they name: vis_mask[b, t] = 1 lets the cells of block b see the headers of block t.
All inputs are finite; a program needn't handle non-finite values.
Results may differ from a plain program's by a relative error of at most 0.012.
Values may be sent and summed in bfloat16 or wider, within the bound.
A program may use at most 64 MiB of HBM per device.

v0:
```python
from functools import partial
import jax
import jax.numpy as jnp
from jax import lax
from jax.sharding import PartitionSpec as P

HD = 128
W = 256
BLOCK = 128
masked_score = -1e30


def product(pattern, former, latter):
    return jnp.einsum(pattern, former, latter, preferred_element_type=jnp.float32)


def block_stats(queries, key_rows, visible, scaling):
    scores = product("nkgd,mkd->kgnm", queries, key_rows) * scaling
    kept_scores = jnp.where(visible, scores, masked_score)
    highest = jnp.max(kept_scores, axis=-1)
    totals = jnp.sum(jnp.where(visible, jnp.exp(scores - highest[..., None]), 0.0), axis=-1)
    return (highest, totals)


def merge_stats(former, latter):
    highest = jnp.maximum(former[0], latter[0])
    return (
        highest,
        former[1] * jnp.exp(former[0] - highest) + latter[1] * jnp.exp(latter[0] - highest),
    )


def weights_of(queries, key_rows, log_totals, visible, scaling):
    scores = product("nkgd,mkd->kgnm", queries, key_rows) * scaling
    return jnp.where(visible, jnp.exp(scores - log_totals[..., None]), 0.0)


def block_delta(queries, grads_out, key_rows, value_rows, log_totals, visible, scaling):
    weights = weights_of(queries, key_rows, log_totals, visible, scaling)
    slopes = product("nkgd,mkd->kgnm", grads_out, value_rows)
    return jnp.sum(weights * slopes, axis=-1)


def block_grads(queries, grads_out, key_rows, value_rows, log_totals, deltas, visible, scaling):
    weights = weights_of(queries, key_rows, log_totals, visible, scaling)
    slopes = product("nkgd,mkd->kgnm", grads_out, value_rows)
    score_grads = weights * (slopes - deltas[..., None])
    weight_low = weights.astype(jnp.bfloat16)
    grad_low = score_grads.astype(jnp.bfloat16)
    grad_values = product("kgnm,nkgd->mkd", weight_low, grads_out)
    grad_keys = product("kgnm,nkgd->mkd", grad_low, queries) * scaling
    grad_queries = product("kgnm,mkd->nkgd", grad_low, key_rows) * scaling
    return (grad_queries, grad_keys, grad_values)


def to_rows(values):
    return jnp.transpose(values, (1, 2, 0, 3)).reshape(values.shape[1], values.shape[2], -1)


def from_rows(values, pieces):
    return jnp.transpose(values.reshape(values.shape[0], values.shape[1], pieces, -1), (2, 0, 1, 3))


def guarded(function, operands):
    return function(*operands)


def per_device(q_cells, k_cells, v_cells, do_cells, q_head, k_head, v_head, do_head, vis_mask):
    cell_count = q_cells.shape[0]
    kv_local = k_cells.shape[1] // HD
    query_local = q_cells.shape[1] // HD
    groups = query_local // kv_local
    scaling = HD ** (-0.5)
    regions = cell_count // W
    own_rows = q_head.shape[0]
    head_keys, head_values = (
        lax.all_gather(k_head, "seq", axis=0, tiled=True),
        lax.all_gather(v_head, "seq", axis=0, tiled=True),
    )
    all_queries, all_grads = (
        lax.all_gather(q_head, "seq", axis=0, tiled=True),
        lax.all_gather(do_head, "seq", axis=0, tiled=True),
    )
    header_count = head_keys.shape[0]
    blocks = header_count // BLOCK
    cell_query = q_cells.reshape(cell_count, kv_local, groups, HD)
    cell_grad = do_cells.reshape(cell_count, kv_local, groups, HD)
    cell_key = k_cells.reshape(cell_count, kv_local, HD)
    cell_value = v_cells.reshape(cell_count, kv_local, HD)
    region_query = q_cells.reshape(regions, W, kv_local, groups, HD)
    region_grad = do_cells.reshape(regions, W, kv_local, groups, HD)
    region_key = k_cells.reshape(regions, W, kv_local, HD)
    region_value = v_cells.reshape(regions, W, kv_local, HD)
    header_key_rows = head_keys.reshape(header_count, kv_local, HD)
    header_value_rows = head_values.reshape(header_count, kv_local, HD)
    key_blocks = head_keys.reshape(blocks, BLOCK, kv_local, HD)
    value_blocks = head_values.reshape(blocks, BLOCK, kv_local, HD)
    seen_blocks = jnp.transpose(jnp.repeat(vis_mask, BLOCK, axis=0) > 0)

    def outer_stat(operands):
        key_block, seen_column = operands
        return guarded(
            partial(block_stats, cell_query, scaling=scaling), (key_block, seen_column[:, None])
        )

    block_highest, block_totals = lax.map(outer_stat, (key_blocks, seen_blocks))
    outer_highest = jnp.max(block_highest, axis=0)
    outer_totals = jnp.sum(block_totals * jnp.exp(block_highest - outer_highest), axis=0)
    local_stats = jax.vmap(partial(block_stats, visible=True, scaling=scaling))(
        region_query, region_key
    )
    highest, totals = merge_stats(
        (to_rows(local_stats[0]), to_rows(local_stats[1])), (outer_highest, outer_totals)
    )
    cell_log = highest + jnp.log(totals)
    region_log = from_rows(cell_log, regions)

    def outer_delta(operands):
        key_block, value_block, seen_column = operands
        return guarded(
            partial(block_delta, cell_query, cell_grad, scaling=scaling),
            (key_block, value_block, cell_log, seen_column[:, None]),
        )

    local_delta = to_rows(
        jax.vmap(partial(block_delta, visible=True, scaling=scaling))(
            region_query, region_grad, region_key, region_value, region_log
        )
    )
    cell_delta = local_delta + jnp.sum(
        lax.map(outer_delta, (key_blocks, value_blocks, seen_blocks)), axis=0
    )
    query_zeros = jnp.zeros((cell_count, kv_local, groups, HD), jnp.float32)

    def outer_grad(running, operands):
        key_block, value_block, seen_column = operands
        gradients = guarded(
            partial(block_grads, cell_query, cell_grad, scaling=scaling),
            (key_block, value_block, cell_log, cell_delta, seen_column[:, None]),
        )
        return (running + gradients[0], (gradients[1], gradients[2]))

    outer_query, (key_parts, value_parts) = lax.scan(
        outer_grad, query_zeros, (key_blocks, value_blocks, seen_blocks)
    )
    local_grads = jax.vmap(partial(block_grads, visible=True, scaling=scaling))(
        region_query,
        region_grad,
        region_key,
        region_value,
        region_log,
        from_rows(cell_delta, regions),
    )
    query_blocks = all_queries.reshape(blocks, BLOCK, kv_local, groups, HD)
    grad_blocks = all_grads.reshape(blocks, BLOCK, kv_local, groups, HD)
    own_query = q_head.reshape(own_rows, kv_local, groups, HD)
    own_grad = do_head.reshape(own_rows, kv_local, groups, HD)
    first_row = lax.axis_index("seq") * own_rows

    def own_slice(values):
        return lax.dynamic_slice_in_dim(values, first_row, own_rows, 2)

    def own_update(values, replaced):
        return lax.dynamic_update_slice_in_dim(values, replaced, first_row, 2)

    cross_stats = lax.map(
        lambda operands: block_stats(operands, cell_key, True, scaling), query_blocks
    )
    cross_highest = to_rows(cross_stats[0])
    cross_totals = to_rows(cross_stats[1])
    self_stats = block_stats(own_query, header_key_rows, True, scaling)
    own_merged = merge_stats((own_slice(cross_highest), own_slice(cross_totals)), self_stats)
    part_highest = own_update(cross_highest, own_merged[0])
    part_totals = own_update(cross_totals, own_merged[1])
    head_highest = lax.pmax(part_highest.astype(jnp.bfloat16), "seq").astype(part_highest.dtype)
    head_totals = lax.psum(part_totals * jnp.exp(part_highest - head_highest), "seq")
    head_log = head_highest + jnp.log(head_totals)
    block_log = from_rows(head_log, blocks)
    own_log = own_slice(head_log)
    cross_delta = to_rows(
        lax.map(
            lambda operands: block_delta(
                operands[0], operands[1], cell_key, cell_value, operands[2], True, scaling
            ),
            (query_blocks, grad_blocks, block_log),
        )
    )
    self_delta = block_delta(
        own_query, own_grad, header_key_rows, header_value_rows, own_log, True, scaling
    )
    part_delta = own_update(cross_delta, own_slice(cross_delta) + self_delta)
    head_delta = lax.psum(part_delta, "seq")
    block_deltas = from_rows(head_delta, blocks)
    own_delta = own_slice(head_delta)
    key_zeros = jnp.zeros((cell_count, kv_local, HD), jnp.float32)

    def cross_grad(running, operands):
        gradients = block_grads(
            operands[0], operands[1], cell_key, cell_value, operands[2], operands[3], True, scaling
        )
        return ((running[0] + gradients[1], running[1] + gradients[2]), gradients[0])

    (cross_key, cross_value), cross_query = lax.scan(
        cross_grad, (key_zeros, key_zeros), (query_blocks, grad_blocks, block_log, block_deltas)
    )
    self_grads = block_grads(
        own_query, own_grad, header_key_rows, header_value_rows, own_log, own_delta, True, scaling
    )
    query_part = cross_query.reshape(header_count, query_local * HD)
    key_part = key_parts.reshape(header_count, kv_local * HD) + self_grads[1].reshape(
        header_count, kv_local * HD
    )
    value_part = value_parts.reshape(header_count, kv_local * HD) + self_grads[2].reshape(
        header_count, kv_local * HD
    )
    whole_sums = lax.psum((query_part, key_part, value_part), "seq")
    query_sum, key_sum, value_sum = [
        lax.dynamic_slice_in_dim(summed, first_row, own_rows, 0) for summed in whole_sums
    ]
    dq_cells = (
        local_grads[0].reshape(cell_count, query_local * HD)
        + outer_query.reshape(cell_count, query_local * HD)
    ).astype(jnp.bfloat16)
    dk_cells = (
        local_grads[1].reshape(cell_count, kv_local * HD)
        + cross_key.reshape(cell_count, kv_local * HD)
    ).astype(jnp.bfloat16)
    dv_cells = (
        local_grads[2].reshape(cell_count, kv_local * HD)
        + cross_value.reshape(cell_count, kv_local * HD)
    ).astype(jnp.bfloat16)
    dq_head = (query_sum + self_grads[0].reshape(own_rows, query_local * HD)).astype(jnp.bfloat16)
    return (
        dq_cells,
        dk_cells,
        dv_cells,
        dq_head,
        key_sum.astype(jnp.bfloat16),
        value_sum.astype(jnp.bfloat16),
    )


def solution(mesh):
    return jax.shard_map(
        per_device,
        mesh=mesh,
        in_specs=(
            P("seq", "head"),
            P("seq", "head"),
            P("seq", "head"),
            P("seq", "head"),
            P("seq", "head"),
            P("seq", "head"),
            P("seq", "head"),
            P("seq", "head"),
            P("seq", None),
        ),
        out_specs=(
            P("seq", "head"),
            P("seq", "head"),
            P("seq", "head"),
            P("seq", "head"),
            P("seq", "head"),
            P("seq", "head"),
        ),
        check_vma=False,
    )
```

profile of v0, /device:TPU:1, one launch (start us, length us, event | category | flops | bytes accessed | tf_op | source)
XLA Modules:
  0.0 988.0 jit_solution(11837171689813258582)
XLA Ops:
  9.5 47.2 %all_gather.12 = bf16[1024,128]{1,0:T(8,128)(2,1)S(1)} all-gather(bf16[32,128]{1,0:T(8,128)(2,1)} %param.26), channel_id=1, replica_groups=mesh['seq'=32,'head'=8] {'seq'}, dimensions={0}, use_global_device_ids=true | all-gather | bytes 270336 | tf_op jit(solution)/shard_map/all_gather | solution.py:77
  56.7 40.4 %all_gather.13 = bf16[1024,128]{1,0:T(8,128)(2,1)} all-gather(bf16[32,128]{1,0:T(8,128)(2,1)} %param.27), channel_id=1, replica_groups=mesh['seq'=32,'head'=8] {'seq'}, dimensions={0}, use_global_device_ids=true | all-gather | bytes 270336 | tf_op jit(solution)/shard_map/all_gather | solution.py:78
  98.7 4.6 while.74
  104.2 1.5 bitcast_reduce_fusion
  109.0 16.5 %while.75 = (s32[]{:T(128)}, f32[8,1,8,256]{3,2,1,0:T(8,128)}, pred[8,256]{1,0:T(8,128)(4,1)S(1)}, bf16[8,128,1,128]{3,1,2,0:T(8,128)(2,1)S(1)}, bf16[256,1,8,12...) while((s32[]{:T(128)}, f32[8,1,8,256]{3,2,1,0:T(8,128)}, ...), condition=%wide.region_11.12_spmd, body=%wide.region_9.11_spmd.sunk | while | flops 135526400 | bytes 3245173 | solution.py:131
  125.5 1.4 reduce_sum.103
  127.8 3.0 fusion.95
  133.0 2.2 copy.97
  135.3 1.9 copy.67
  137.2 37.2 %all-gather.5.cloned.1.call-done = bf16[1024,1024]{1,0:T(8,128)(2,1)} async-done(((bf16[32,1024]{1,0:T(8,128)(2,1)}), bf16[1024,1024]{1,0:T(8,128)(2,1)}) %all-gather.5.cloned.1.call-update) | async-done | bytes 2097168 | tf_op jit(solution)/shard_map/all_gather | solution.py:82
  174.4 2.2 copy.98
  176.6 1.9 copy.68
  179.8 18.8 %while.76 = (s32[]{:T(128)}, f32[8,1,8,128]{3,2,1,0:T(8,128)}, f32[8,1,8,128]{3,2,1,0:T(8,128)}, bf16[8,128,1,8,128]{4,1,3,2,0:T(8,128)(2,1)}, bf16[256,1,128]{2,0,1:T(8,128)(2,1)S(1)}, /*index=5*/s32[]{:T(128)}) while((s32[]{:T(128)}, f32[8,1,8,128]{3,2,1,0:T(8,128)}, f32[8,1,8,128]{3,2,1,0:T(8,128)}, ...), condition=%wide.region_18.19_spmd, body=%wide.region_15.18_spmd.sunk | while | flops 68155392 | bytes 2453589 | solution.py:166
  179.8 1.4 fusion.227
  182.1 1.3 fusion.227
  184.5 1.3 fusion.227
  186.8 1.4 fusion.227
  189.1 1.3 fusion.227
  191.5 1.3 fusion.227
  193.8 1.3 fusion.227
  196.2 1.4 fusion.227
  198.5 1.4 fusion.157
  199.9 1.5 dynamic_update_slice.41
  201.4 1.5 dynamic_update_slice.40
  202.8 1.4 convert_element_type.50
  204.2 124.3 %pmax.7 = bf16[1,8,1024]{2,1,0:T(8,128)(2,1)} all-reduce(bf16[1,8,1024]{2,1,0:T(8,128)(2,1)} %convert_element_type.50), channel_id=1, replica_groups=mesh['seq'=32,'head'=8] {'seq'}, use_global_device_ids=true, to_apply=%region_20.21 | all-reduce | flops 8192 | bytes 32768 | tf_op jit(solution)/shard_map/pmax | solution.py:175
  328.5 1.4 fusion.148
  329.9 128.5 %psum.35 = f32[1,8,1024]{2,1,0:T(8,128)} all-reduce(f32[1,8,1024]{2,1,0:T(8,128)} %fusion.148), channel_id=1, replica_groups=mesh['seq'=32,'head'=8] {'seq'}, use_global_device_ids=true, to_apply=%region_22.23 | all-reduce | flops 8192 | bytes 65536 | tf_op jit(solution)/shard_map/psum | solution.py:176
  460.5 31.5 %while.77 = (s32[]{:T(128)}, f32[8,1,8,128]{3,2,1,0:T(8,128)}, bf16[8,128,1,8,128]{4,1,3,2,0:T(8,128)(2,1)}, bf16[256,1,128]{2,0,1:T(8,128)(2,1)S(1)}, f32[8,1,8...) while((s32[]{:T(128)}, f32[8,1,8,128]{3,2,1,0:T(8,128)}, ...), condition=%wide.region_25.26_spmd, body=%wide.region_23.25_spmd.sunk | while | flops 135265280 | bytes 2777197 | solution.py:181
  462.4 1.4 fusion.233
  466.4 1.4 fusion.233
  470.3 1.4 fusion.233
  474.2 1.4 fusion.233
  478.2 1.4 fusion.233
  482.1 1.4 fusion.233
  486.0 1.4 fusion.233
  490.0 1.4 fusion.233
  491.9 2.6 multiply_reduce_fusion
  494.5 1.4 bitcast_add_fusion.1
  495.9 1.5 dynamic_update_slice.42
  497.3 128.5 %psum.36 = f32[1,8,1024]{2,1,0:T(8,128)} all-reduce(f32[1,8,1024]{2,1,0:T(8,128)} %dynamic_update_slice.42), channel_id=1, replica_groups=mesh['seq'=32,'head'=8] {'seq'}, use_global_device_ids=true, to_apply=%region_27.28 | all-reduce | flops 8192 | bytes 65536 | tf_op jit(solution)/shard_map/psum | solution.py:192
  625.9 63.3 %while.79 = (s32[]{:T(128)}, f32[256,1,128]{0,2,1:T(8,128)}, f32[256,1,128]{0,2,1:T(8,128)}, f32[8,128,1,8,128]{4,3,1,0,2:T(8,128)}, bf16[8,128,1,8,128]{4,1,3,2...) while((s32[]{:T(128)}, f32[256,1,128]{0,2,1:T(8,128)}, ...), condition=%wide.region_29.30_spmd.clone, body=%wide.region_28.29_spmd.clone.sunk | while | flops 337412096 | bytes 9134296 | solution.py:203
  627.9 1.9 fusion.262
  635.8 1.9 fusion.262
  642.4 1.3 fusion.259
  643.7 1.9 fusion.262
  650.3 1.3 fusion.259
  651.6 1.9 fusion.262
  658.2 1.3 fusion.259
  659.5 1.9 fusion.262
  667.4 1.9 fusion.262
  675.4 1.9 fusion.262
  683.3 1.9 fusion.262
  689.2 5.1 copy.144
  694.9 39.1 %while.78 = (s32[]{:T(128)}, f32[256,1,8,128]{0,3,2,1:T(8,128)}, f32[8,128,1,128]{3,1,2,0:T(8,128)}, f32[8,128,1,128]{3,1,2,0:T(8,128)}, bf16[8,128,1,128]{3,1,2...) while((s32[]{:T(128)}, f32[256,1,8,128]{0,3,2,1:T(8,128)}, ...), condition=%wide.region_14.15_spmd.clone, body=%wide.region_13.14_spmd.clone.sunk | while | flops 338182144 | bytes 17548512 | solution.py:143
  734.1 2.5 copy.83
  736.6 2.1 fusion.114
  738.7 1.4 convolution_multiply_fusion.8
  740.1 2.5 copy.60
  742.7 2.6 add_convert_fusion
  749.5 140.0 %all-reduce.5 = (bf16[1024,128]{1,0:T(8,128)(2,1)S(1)}, bf16[1024,128]{1,0:T(8,128)(2,1)}) all-reduce(f32[1024,128]{1,0:T(8,128)} %fusion.104, f32[1024,128]{1,0:T(8,128)} %fusion.105), channel_id=1, replica_groups=mesh['seq'=32,'head'=8] {'seq'}, use_global_device_ids=true, to_apply=%region_31.32 | all-reduce | flops 262144 | bytes 1572864 | tf_op jit(solution)/shard_map/psum | solution.py:216
  890.8 2.4 fusion.111
  894.4 85.6 %all-reduce.4.cloned.1.call-done = f32[1024,1024]{1,0:T(8,128)} async-done(((f32[1024,1024]{1,0:T(8,128)}), f32[1024,1024]{1,0:T(8,128)}) %all-reduce.4.cloned.1.call-update) | async-done | bytes 4194320 | tf_op jit(solution)/shard_map/psum | solution.py:216
  979.9 1.6 fusion.135
  (362 shorter events, 153.0 us)
Async XLA Ops:
  7.2 125.9 %all-gather.3.cloned.1.call-start = ((), (), s32[]{:S(2)}) async-start(), calls=%async_computation | async-start | bytes 2162688 | tf_op jit(solution)/shard_map/all_gather | solution.py:81
  7.9 166.5 %all-gather.5.cloned.1.call-start = ((), (), s32[]{:S(2)}) async-start(), calls=%async_computation.1 | async-start | bytes 2162688 | tf_op jit(solution)/shard_map/all_gather | solution.py:82
  8.6 971.3 %all-reduce.4.cloned.1.call-start = ((), (), s32[]{:S(2)}) async-start(), calls=%async_computation.2 | async-start | bytes 8388608 | tf_op jit(solution)/shard_map/psum | solution.py:216
  98.7 4.6 copy-start.9
  103.3 0.6 copy-start.15
  103.3 0.9 copy-start.2
  105.7 1.5 copy-start.23
  106.4 1.3 copy-start.24
  107.2 1.8 copy-start.26
  107.6 1.4 copy-start.25
  109.0 18.7 %copy-start.5 = (bf16[256,128]{1,0:T(8,128)(2,1)S(1)}, bf16[256,128]{1,0:T(8,128)(2,1)}, u32[]{:S(2)}) copy-start(bf16[256,128]{1,0:T(8,128)(2,1)} %param.23) | copy-start | bytes 196612
  125.5 5.2 copy-start.19
  127.8 3.0 copy-start.21
  127.8 3.0 copy-start.29
  127.8 3.0 copy-start.16
  131.2 1.0 copy-start.3
  131.2 1.0 copy-start.27
  459.2 1.3 copy-start.18
  626.6 4.5 copy-start.6
  632.3 1.4 copy-start.7
  634.5 4.5 copy-start.6
  640.2 1.4 copy-start.7
  642.4 4.5 copy-start.6
  648.2 1.4 copy-start.7
  650.3 4.5 copy-start.6
  656.1 1.4 copy-start.7
  658.2 4.5 copy-start.6
  664.0 1.4 copy-start.7
  666.1 4.5 copy-start.6
  671.9 1.4 copy-start.7
  674.1 4.5 copy-start.6
  679.8 1.4 copy-start.7
  682.0 4.5 copy-start.6
  687.7 1.4 copy-start.7
  694.3 0.7 copy-start.20
  695.3 3.0 copy-start
  698.8 1.1 copy-start.1
  700.2 3.0 copy-start
  703.7 1.1 copy-start.1
  705.1 3.0 copy-start
  708.6 1.1 copy-start.1
  710.0 3.0 copy-start
  713.5 1.1 copy-start.1
  714.9 3.0 copy-start
  718.3 1.1 copy-start.1
  719.8 3.0 copy-start
  723.2 1.1 copy-start.1
  724.7 3.0 copy-start
  728.1 1.1 copy-start.1
  729.6 3.0 copy-start
  733.0 1.1 copy-start.1
  734.1 2.5 copy-start.22
  738.7 1.4 copy-start.12
  740.1 6.0 copy-start.28
  742.7 3.5 copy-start.4
  742.7 3.5 copy-start.13
  745.3 1.5 copy-start.17
  745.3 1.5 copy-start.31
  746.4 1.6 copy-start.14
  746.5 1.6 copy-start.30
  746.9 2.4 copy-start.8
  746.9 2.5 copy-start.11
  749.3 143.9 %copy-start.10 = (bf16[256,1024]{1,0:T(8,128)(2,1)S(1)}, bf16[256,1024]{1,0:T(8,128)(2,1)}, u32[]{:S(2)}) copy-start(bf16[256,1024]{1,0:T(8,128)(2,1)} %param.24) | copy-start | bytes 1572868
Sparse Core Ops, SparseCore 0:
  10.8 84.3 all-gather.2
  98.0 76.3 all-gather.4
  694.4 285.4 all-reduce.3
where the time goes:
time: 992 us; the launch traced here: 988 us
  blocking collectives  609 us (61%)
  matrix products  139 us (14%)
  waiting for transfers between devices  124 us (12%)
  local copies, waits for them, and re-layouts  76.3 us (8%)
  other arithmetic  23.8 us (2%)
  between operations  14.2 us (1%)
    psum x1, blocking collectives, per_device(): whole_sums = lax.psum((query_part, key_part, value_part), 'seq')  140 us
    dot_general x138, matrix products, product(): jnp.einsum(pattern, former, latter, preferred_element_type=jnp.float32)  139 us
    psum x1, blocking collectives, per_device(): head_delta = lax.psum(part_delta, 'seq')  129 us
    psum x1, blocking collectives, per_device(): lax.psum(part_totals * jnp.exp(part_highest - head_highest), 'seq')  128 us
    pmax x1, blocking collectives, per_device(): lax.pmax(part_highest.astype(jnp.bfloat16), 'seq')  124 us
    psum x1, waiting for transfers between devices, per_device(): whole_sums = lax.psum((query_part, key_part, value_part), 'seq')  85.6 us
    all_gather x1, blocking collectives, per_device(): lax.all_gather(k_head, 'seq', axis=0, tiled=True)  47.2 us
    all_gather x1, blocking collectives, per_device(): lax.all_gather(v_head, 'seq', axis=0, tiled=True)  40.4 us
  transfers between devices with their start and end apart: 3, of which 2 were waited for; matrix products, arithmetic and copies ran while one was open for 9% of the time, Pallas kernels for 0%

commit v1 on v0

--- a/solution.py
+++ b/solution.py
@@ -189,7 +189,7 @@
         own_query, own_grad, header_key_rows, header_value_rows, own_log, True, scaling
     )
     part_delta = own_update(cross_delta, own_slice(cross_delta) + self_delta)
-    head_delta = lax.psum(part_delta, "seq")
+    head_delta = jnp.sum(lax.all_gather(part_delta, "seq"), axis=0)
     block_deltas = from_rows(head_delta, blocks)
     own_delta = own_slice(head_delta)
     key_zeros = jnp.zeros((cell_count, kv_local, HD), jnp.float32)

time: 992 us -> 938 us (0.946)
  blocking collectives: 609 us -> 478 us
  waiting for transfers between devices: 124 us -> 202 us
    psum x1 -> x0, blocking collectives: 129 us -> none  [per_device(): head_delta = lax.psum(part_delta, 'seq')]
    all_gather x0 -> x1, waiting for transfers between devices: none -> 59.4 us  [per_device(): head_delta = jnp.sum(lax.all_gather(part_delta, 'seq'), axis=0)]
    all_gather x1, waiting for transfers between devices: 37.2 us -> 62.3 us  [per_device(): lax.all_gather(do_head, 'seq', axis=0, tiled=True)]
  transfers between devices with their start and end apart: 3 -> 4, of which waited for: 2 -> 3; matrix products, arithmetic and copies ran while one was open for 9% -> 9% of each run, Pallas kernels for 0% -> 0%
where the time goes in v1:
time: 938 us; the launch traced here: 934 us
  blocking collectives  478 us (51%)
  waiting for transfers between devices  202 us (22%)
  matrix products  139 us (15%)
  local copies, waits for them, and re-layouts  75.7 us (8%)
  other arithmetic  22.9 us (2%)
  between operations  14.2 us (2%)
    dot_general x138, matrix products, product(): jnp.einsum(pattern, former, latter, preferred_element_type=jnp.float32)  139 us
    psum x1, blocking collectives, per_device(): whole_sums = lax.psum((query_part, key_part, value_part), 'seq')  138 us
    psum x1, blocking collectives, per_device(): lax.psum(part_totals * jnp.exp(part_highest - head_highest), 'seq')  128 us
    pmax x1, blocking collectives, per_device(): lax.pmax(part_highest.astype(jnp.bfloat16), 'seq')  124 us
    psum x1, waiting for transfers between devices, per_device(): whole_sums = lax.psum((query_part, key_part, value_part), 'seq')  79.4 us
    all_gather x1, waiting for transfers between devices, per_device(): lax.all_gather(do_head, 'seq', axis=0, tiled=True)  62.3 us
    all_gather x1, waiting for transfers between devices, per_device(): head_delta = jnp.sum(lax.all_gather(part_delta, 'seq'), axis=0)  59.4 us
    all_gather x1, blocking collectives, per_device(): lax.all_gather(k_head, 'seq', axis=0, tiled=True)  47.2 us
  transfers between devices with their start and end apart: 4, of which 3 were waited for; matrix products, arithmetic and copies ran while one was open for 9% of the time, Pallas kernels for 0%

profile of v1, /device:TPU:1, one launch (start us, length us, event | category | flops | bytes accessed | tf_op | source)
XLA Modules:
  0.0 934.0 jit_solution(4103294388342723394)
XLA Ops:
  9.5 47.2 %all_gather.20 = bf16[1024,128]{1,0:T(8,128)(2,1)S(1)} all-gather(bf16[32,128]{1,0:T(8,128)(2,1)} %param.26), channel_id=1, replica_groups=mesh['seq'=32,'head'=8] {'seq'}, dimensions={0}, use_global_device_ids=true | all-gather | bytes 270336 | tf_op jit(solution)/shard_map/all_gather | solution.py:77
  58.7 4.6 while.74
  63.4 40.1 %all_gather.21 = bf16[1024,128]{1,0:T(8,128)(2,1)} all-gather(bf16[32,128]{1,0:T(8,128)(2,1)S(1)} %copy-done.30), channel_id=1, replica_groups=mesh['seq'=32,'head'=8] {'seq'}, dimensions={0}, use_global_device_ids=true | all-gather | bytes 270336 | tf_op jit(solution)/shard_map/all_gather | solution.py:78
  105.8 1.5 bitcast_reduce_fusion
  108.1 2.2 copy.135
  110.3 1.9 copy.104
  112.2 62.3 %all-gather.6.cloned.1.call-done = bf16[1024,1024]{1,0:T(8,128)(2,1)} async-done(((bf16[32,1024]{1,0:T(8,128)(2,1)}), bf16[1024,1024]{1,0:T(8,128)(2,1)}) %all-gather.6.cloned.1.call-update) | async-done | bytes 2097168 | tf_op jit(solution)/shard_map/all_gather | solution.py:82
  174.5 2.2 copy.136
  176.8 1.9 copy.105
  179.9 18.8 %while.76 = (s32[]{:T(128)}, f32[8,1,8,128]{3,2,1,0:T(8,128)}, f32[8,1,8,128]{3,2,1,0:T(8,128)}, bf16[8,128,1,8,128]{4,1,3,2,0:T(8,128)(2,1)}, bf16[256,1,128]{2,0,1:T(8,128)(2,1)S(1)}, /*index=5*/s32[]{:T(128)}) while((s32[]{:T(128)}, f32[8,1,8,128]{3,2,1,0:T(8,128)}, f32[8,1,8,128]{3,2,1,0:T(8,128)}, ...), condition=%wide.region_18.19_spmd, body=%wide.region_15.18_spmd.sunk | while | flops 68155392 | bytes 2453589 | solution.py:166
  179.9 1.4 fusion.228
  182.3 1.3 fusion.228
  184.6 1.4 fusion.228
  186.9 1.4 fusion.228
  189.3 1.4 fusion.228
  191.6 1.4 fusion.228
  194.0 1.4 fusion.228
  196.3 1.4 fusion.228
  198.7 1.4 fusion.158
  200.1 1.5 dynamic_update_slice.42
  201.5 1.5 dynamic_update_slice.41
  203.0 1.4 convert_element_type.50
  204.4 124.3 %pmax.7 = bf16[1,8,1024]{2,1,0:T(8,128)(2,1)} all-reduce(bf16[1,8,1024]{2,1,0:T(8,128)(2,1)} %convert_element_type.50), channel_id=1, replica_groups=mesh['seq'=32,'head'=8] {'seq'}, use_global_device_ids=true, to_apply=%region_20.21 | all-reduce | flops 8192 | bytes 32768 | tf_op jit(solution)/shard_map/pmax | solution.py:175
  328.6 1.4 fusion.148
  330.0 128.5 %psum.28 = f32[1,8,1024]{2,1,0:T(8,128)} all-reduce(f32[1,8,1024]{2,1,0:T(8,128)} %fusion.148), channel_id=1, replica_groups=mesh['seq'=32,'head'=8] {'seq'}, use_global_device_ids=true, to_apply=%region_22.23 | all-reduce | flops 8192 | bytes 65536 | tf_op jit(solution)/shard_map/psum | solution.py:176
  460.0 31.5 %while.77 = (s32[]{:T(128)}, f32[8,1,8,128]{3,2,1,0:T(8,128)}, bf16[8,128,1,8,128]{4,1,3,2,0:T(8,128)(2,1)}, bf16[256,1,128]{2,0,1:T(8,128)(2,1)S(1)}, f32[8,1,8...) while((s32[]{:T(128)}, f32[8,1,8,128]{3,2,1,0:T(8,128)}, ...), condition=%wide.region_25.26_spmd, body=%wide.region_23.25_spmd.sunk | while | flops 135265280 | bytes 2777197 | solution.py:181
  462.0 1.4 fusion.234
  465.9 1.4 fusion.234
  469.8 1.4 fusion.234
  473.8 1.4 fusion.234
  477.7 1.4 fusion.234
  481.6 1.4 fusion.234
  485.6 1.4 fusion.234
  489.5 1.4 fusion.234
  491.5 2.6 multiply_reduce_fusion
  494.8 1.4 dynamic_update_slice.43
  497.2 16.5 %while.75 = (s32[]{:T(128)}, f32[8,1,8,256]{3,2,1,0:T(8,128)}, pred[8,256]{1,0:T(8,128)(4,1)S(1)}, bf16[8,128,1,128]{3,1,2,0:T(8,128)(2,1)S(1)}, bf16[256,1,8,12...) while((s32[]{:T(128)}, f32[8,1,8,256]{3,2,1,0:T(8,128)}, ...), condition=%wide.region_11.12_spmd, body=%wide.region_9.11_spmd.sunk | while | flops 135526400 | bytes 3245173 | solution.py:131
  513.7 1.4 reduce_sum.112
  515.9 3.0 fusion.95
  518.9 59.4 %all-gather.8.cloned.1.call-done = f32[32,1,8,1024]{3,2,1,0:T(8,128)} async-done(((f32[1,1,8,1024]{3,2,1,0:T(8,128)}), f32[32,1,8,1024]{3,2,1,0:T(8,128)}) %all-gather.8.cloned.1.call-update) | async-done | bytes 1048592 | tf_op jit(solution)/shard_map/all_gather | solution.py:192
  578.3 1.9 reduce_sum.117
  580.2 63.3 %while.79 = (s32[]{:T(128)}, f32[256,1,128]{0,2,1:T(8,128)}, f32[256,1,128]{0,2,1:T(8,128)}, f32[8,128,1,8,128]{4,3,1,0,2:T(8,128)}, bf16[8,128,1,8,128]{4,1,3,2...) while((s32[]{:T(128)}, f32[256,1,128]{0,2,1:T(8,128)}, ...), condition=%wide.region_29.30_spmd.clone, body=%wide.region_28.29_spmd.clone.sunk | while | flops 337412096 | bytes 9134296 | solution.py:203
  582.2 1.9 fusion.263
  588.8 1.3 fusion.260
  590.1 1.9 fusion.263
  596.7 1.3 fusion.260
  598.0 1.9 fusion.263
  605.9 1.9 fusion.263
  613.9 1.9 fusion.263
  621.8 1.9 fusion.263
  629.7 1.9 fusion.263
  636.3 1.3 fusion.260
  637.6 1.9 fusion.263
  643.5 5.1 copy.182
  649.2 39.1 %while.78 = (s32[]{:T(128)}, f32[256,1,8,128]{0,3,2,1:T(8,128)}, f32[8,128,1,128]{3,1,2,0:T(8,128)}, f32[8,128,1,128]{3,1,2,0:T(8,128)}, bf16[8,128,1,128]{3,1,2...) while((s32[]{:T(128)}, f32[256,1,8,128]{0,3,2,1:T(8,128)}, ...), condition=%wide.region_14.15_spmd.clone, body=%wide.region_13.14_spmd.clone.sunk | while | flops 338182144 | bytes 17548512 | solution.py:143
  688.4 2.5 copy.120
  690.9 2.1 fusion.114
  693.0 1.4 convolution_multiply_fusion.8
  694.4 2.6 copy.97
  697.0 2.6 add_convert_fusion
  703.8 137.9 %all-reduce.5 = (bf16[1024,128]{1,0:T(8,128)(2,1)S(1)}, bf16[1024,128]{1,0:T(8,128)(2,1)}) all-reduce(f32[1024,128]{1,0:T(8,128)} %fusion.104, f32[1024,128]{1,0:T(8,128)} %fusion.105), channel_id=1, replica_groups=mesh['seq'=32,'head'=8] {'seq'}, use_global_device_ids=true, to_apply=%region_31.32 | all-reduce | flops 262144 | bytes 1572864 | tf_op jit(solution)/shard_map/psum | solution.py:216
  843.0 2.4 fusion.111
  846.6 79.4 %all-reduce.4.cloned.1.call-done = f32[1024,1024]{1,0:T(8,128)} async-done(((f32[1024,1024]{1,0:T(8,128)}), f32[1024,1024]{1,0:T(8,128)}) %all-reduce.4.cloned.1.call-update) | async-done | bytes 4194320 | tf_op jit(solution)/shard_map/psum | solution.py:216
  926.0 1.6 fusion.135
  (367 shorter events, 151.2 us)
Async XLA Ops:
  7.2 51.0 %copy-start.9 = (bf16[256,1024]{1,0:T(8,128)(2,1)S(1)}, bf16[256,1024]{1,0:T(8,128)(2,1)}, u32[]{:S(2)}) copy-start(bf16[256,1024]{1,0:T(8,128)(2,1)} %param.24) | copy-start | bytes 1572868
  7.2 100.9 %all-gather.4.cloned.1.call-start = ((), (), s32[]{:S(2)}) async-start(), calls=%async_computation | async-start | bytes 2162688 | tf_op jit(solution)/shard_map/all_gather | solution.py:81
  7.9 166.6 %all-gather.6.cloned.1.call-start = ((), (), s32[]{:S(2)}) async-start(), calls=%async_computation.1 | async-start | bytes 2162688 | tf_op jit(solution)/shard_map/all_gather | solution.py:82
  8.7 569.6 %all-gather.8.cloned.1.call-start = ((), (), s32[]{:S(2)}) async-start(), calls=%async_computation.2 | async-start | bytes 1081344 | tf_op jit(solution)/shard_map/all_gather | solution.py:192
  58.7 4.7 copy-start.30
  58.7 44.8 %copy-start.15 = (bf16[32,1024]{1,0:T(8,128)(2,1)S(1)}, bf16[32,1024]{1,0:T(8,128)(2,1)}, u32[]{:S(2)}) copy-start(bf16[32,1024]{1,0:T(8,128)(2,1)} %param.25) | copy-start | bytes 196612
  63.3 42.5 %copy-start.2 = (bf16[256,128]{1,0:T(8,128)(2,1)S(1)}, bf16[256,128]{1,0:T(8,128)(2,1)}, u32[]{:S(2)}) copy-start(bf16[256,128]{1,0:T(8,128)(2,1)} %param.22) | copy-start | bytes 196612
  63.4 43.9 %copy-start.23 = (f32[8,256]{1,0:T(8,128)}, f32[8,256]{1,0:T(8,128)S(1)}, u32[]{:S(2)}) copy-start(f32[8,256]{1,0:T(8,128)S(1)} %reduce_max.52) | copy-start | bytes 24580
  63.4 44.3 %copy-start.26 = (f32[8,256]{1,0:T(8,128)}, f32[8,256]{1,0:T(8,128)S(1)}, u32[]{:S(2)}) copy-start(f32[8,256]{1,0:T(8,128)S(1)} %multiply_reduce_fusion.1) | copy-start | bytes 24580
  103.9 1.0 copy-start.3
  107.3 3.0 copy-start.22
  107.3 0.7 copy-start.24
  108.0 2.3 copy-start.25
  179.9 280.1 %copy-start.5 = (bf16[256,128]{1,0:T(8,128)(2,1)S(1)}, bf16[256,128]{1,0:T(8,128)(2,1)}, u32[]{:S(2)}) copy-start(bf16[256,128]{1,0:T(8,128)(2,1)} %param.23) | copy-start | bytes 196612
  459.3 0.7 copy-start.17
  459.4 32.1 %copy-start.27 = (f32[8,32]{1,0:T(8,128)}, f32[8,32]{1,0:T(8,128)S(1)}, u32[]{:S(2)}) copy-start(f32[8,32]{1,0:T(8,128)S(1)} %dynamic-slice_bitcast_fusion.3) | copy-start | bytes 3076
  496.3 429.7 %all-reduce.4.cloned.1.call-start = ((), (), s32[]{:S(2)}) async-start(), calls=%async_computation.3 | async-start | bytes 8388608 | tf_op jit(solution)/shard_map/psum | solution.py:216
  513.7 5.2 copy-start.18
  515.9 3.0 copy-start.20
  515.9 3.0 copy-start.29
  580.9 4.5 copy-start.6
  586.7 1.4 copy-start.7
  588.8 4.5 copy-start.6
  594.6 1.4 copy-start.7
  596.7 4.5 copy-start.6
  602.5 1.4 copy-start.7
  604.6 4.5 copy-start.6
  610.4 1.4 copy-start.7
  612.5 4.5 copy-start.6
  618.3 1.4 copy-start.7
  620.5 4.5 copy-start.6
  626.2 1.4 copy-start.7
  628.4 4.5 copy-start.6
  634.1 1.4 copy-start.7
  636.3 4.5 copy-start.6
  642.0 1.4 copy-start.7
  649.6 3.0 copy-start
  653.1 1.1 copy-start.1
  654.5 3.0 copy-start
  657.9 1.1 copy-start.1
  659.4 3.0 copy-start
  662.9 1.1 copy-start.1
  664.3 3.0 copy-start
  667.8 1.1 copy-start.1
  669.2 3.0 copy-start
  672.6 1.1 copy-start.1
  674.1 3.0 copy-start
  677.5 1.1 copy-start.1
  679.0 3.0 copy-start
  682.4 1.1 copy-start.1
  683.8 3.0 copy-start
  687.3 1.1 copy-start.1
  688.4 2.5 copy-start.21
  693.0 1.4 copy-start.12
  694.4 5.2 copy-start.4
  694.4 5.2 copy-start.14
  694.4 5.2 copy-start.28
  697.0 2.6 copy-start.31
  697.0 4.7 copy-start.13
  700.9 1.5 copy-start.16
  700.9 1.5 copy-start.32
  702.0 1.6 copy-start.8
  702.0 1.7 copy-start.11
  703.6 141.8 %copy-start.10 = (bf16[256,1024]{1,0:T(8,128)(2,1)S(1)}, bf16[256,1024]{1,0:T(8,128)(2,1)}, u32[]{:S(2)}) copy-start(bf16[256,1024]{1,0:T(8,128)(2,1)} %param.24) | copy-start | bytes 1572868
  (1 other events, 0.6 us)
Sparse Core Ops, SparseCore 0:
  10.8 84.3 all-gather.3
  98.0 76.5 all-gather.5
  496.4 81.8 all-gather.7
  648.7 277.1 all-reduce.3
